TPU v7x, 32 devices: a whole 2x2x4 slice. The times are simulated.
32 devices in a mesh: slab: 8 (over z, y), sub: 4 (over x, core).
Axes of the slice: x: 2, y: 2, z: 4, core: 2. Of those that a mesh axis runs over, the one named last changes fastest.
Arguments:
- coefficients: bfloat16 [7, 6, 6, 64, 12, 128], P(None, None, None, 'slab', 'sub'), may hold values from -1 to 1
- earlier: float32 [30, 6, 64, 12, 128], P(None, None, 'slab', 'sub'), may hold values from -6 to 6
- start: float32 [6, 64, 12, 128], P(None, 'slab', 'sub'), may hold values from -8 to 8
- shifts: float32 [5], replicated, may hold values from -0.3 to 0.3
Outputs:
- new_basis: float32 [6, 6, 64, 12, 128], P(None, None, 'slab', 'sub')
- projection: float32 [30, 6], replicated
- triangle: float32 [6, 6], replicated
All inputs are finite; a program needn't handle non-finite values.
Results may differ from a plain program's by a relative error of at most 0.0015.
Values may be sent and summed in bfloat16 or wider, within the bound.
A program may use at most 64 MiB of HBM per device.

v0:
```python
import jax
import jax.numpy as jnp
from jax import lax
from jax.sharding import PartitionSpec as P


def padded_2(block, sides, width):
    for axis, dim in sides:
        count = lax.axis_size(axis)
        forward = [(i, i + 1) for i in range(count - 1)]
        backward = [(target, source) for source, target in forward]
        low = lax.ppermute(
            lax.slice_in_dim(block, block.shape[dim] - width, None, axis=dim), axis, forward
        )
        high = lax.ppermute(lax.slice_in_dim(block, 0, width, axis=dim), axis, backward)
        block = jnp.concatenate([low, block, high], axis=dim)
    return block


def nearby_fields(padded):
    center = padded[:, 1:-1, 1:-1]
    zeros_edge = jnp.zeros_like(center[..., :1])
    lower_y = jnp.concatenate([zeros_edge, center[..., :-1]], axis=3)
    upper_y = jnp.concatenate([center[..., 1:], zeros_edge], axis=3)
    return [
        center,
        padded[:, :-2, 1:-1],
        padded[:, 2:, 1:-1],
        padded[:, 1:-1, :-2],
        padded[:, 1:-1, 2:],
        lower_y,
        upper_y,
    ]


def apply_padded(coefficients, padded, theta):
    fields = nearby_fields(padded)
    result = (1.0 - theta) * fields[0]
    for coupling in range(len(fields)):
        result = result + jnp.sum(coefficients[coupling] * fields[coupling][None], axis=1)
    return result


def body(coefficients, earlier, start, shifts):
    depth = shifts.shape[0]
    vectors = [start]
    current = padded_2(start, (("slab", 1),), depth)
    wide_coefficients = padded_2(coefficients, (("slab", 3),), depth)
    for step in range(depth):
        beside = padded_2(current, (("sub", 2),), 1)
        padded = jnp.pad(beside, ((0, 0), (1, 1), (0, 0), (0, 0)))
        current = apply_padded(wide_coefficients, padded, shifts[step])
        vectors.append(current[:, depth:-depth])
    basis = jnp.stack(vectors)
    block_count = basis.shape[0]
    flat = basis.reshape(block_count, -1)
    earlier_flat = earlier.reshape(earlier.shape[0], -1)
    count = flat.shape[1] * lax.axis_size("slab") * lax.axis_size("sub")
    local_cross = jnp.dot(earlier_flat, flat.T, precision=lax.Precision.HIGHEST)
    local_self = jnp.dot(flat, flat.T, precision=lax.Precision.HIGHEST)
    local_earlier = jnp.dot(earlier_flat, earlier_flat.T, precision=lax.Precision.HIGHEST)
    cross_sum, self_sum, earlier_sum = lax.psum(
        (local_cross, local_self, local_earlier), ("slab", "sub")
    )
    projection = cross_sum / count
    rest = flat - jnp.dot(projection.T, earlier_flat, precision=lax.Precision.HIGHEST)
    weighted = jnp.dot(earlier_sum / count, projection, precision=lax.Precision.HIGHEST)
    gram = self_sum / count - 2.0 * jnp.dot(
        projection.T, projection, precision=lax.Precision.HIGHEST
    )
    gram = gram + jnp.dot(projection.T, weighted, precision=lax.Precision.HIGHEST)
    lower = jnp.linalg.cholesky(gram)
    new_flat = lax.linalg.triangular_solve(lower, rest, left_side=True, lower=True)
    return (new_flat.reshape(basis.shape), projection, lower.T)


def solution(mesh):
    placed = (
        P(None, None, None, "slab", "sub", None),
        P(None, None, "slab", "sub", None),
        P(None, "slab", "sub", None),
        P(),
    )
    return jax.shard_map(
        body,
        mesh=mesh,
        in_specs=placed,
        out_specs=(P(None, None, "slab", "sub", None), P(), P()),
        check_vma=False,
    )
```

profile of v0, /device:TPU:0, one launch (start us, length us, event | category | flops | bytes accessed | tf_op | source)
XLA Modules:
  0.0 177.3 jit_solution(12425602278455781404)
XLA Ops:
  0.6 1.0 fusion.71
  1.6 1.3 collective-permute-start.1
  2.9 5.5 %collective-permute-start = (f32[6,5,3,128]{3,1,2,0:T(8,128)S(1)}, f32[6,5,3,128]{3,1,2,0:T(8,128)S(1)}, u32[]{:S(2)}, u32[]{:S(2)}) collective-permute-start(f32[6,5,3,128]{3,1,2,0:T(8,128)S(1)} %get-tuple-element.112), channel_id=1, source_target_pairs={{0,4},{4,8},{8,12},{12,16},{16,20},{20,24},{24,28},{1,5},{5,9},{9,... | collective-permute-start | bytes 138248 | tf_op jit(solution)/shard_map/ppermute | solution.py:12
  8.4 2.5 %fusion.55 = (bf16[7,6,6,5,3,128]{5,3,4,2,1,0:T(8,128)(2,1)S(1)}, bf16[7,6,6,5,3,128]{5,3,4,2,1,0:T(8,128)(2,1)S(1)}) fusion(bf16[7,6,6,8,3,128]{5,3,4,2,1,0:T(8,128)(2,1)} %param.4), kind=kLoop, calls=%fused_computation.150 | loop fusion | bytes 3870720 | tf_op jit(solution)/shard_map/slice | solution.py:13
  10.9 1.5 copy.352
  12.4 1.3 collective-permute-start.3
  13.7 1.5 copy.351
  15.2 6.6 %collective-permute-start.2 = (bf16[7,6,6,5,3,128]{5,0,4,3,2,1:T(8,128)(2,1)}, bf16[7,6,6,5,3,128]{5,0,4,3,2,1:T(8,128)(2,1)}, u32[]{:S(2)}, u32[]{:S(2)}) collective-permute-start(bf16[7,6,6,5,3,128]{5,0,4,3,2,1:T(8,128)(2,1)} %copy.351), channel_id=1, source_target_pairs={{0,4},{4,8},{8,12},{12,16},{16,20},{20,24},{24,28},{1,5},{5,9},{9,... | collective-permute-start | bytes 2903048 | tf_op jit(solution)/shard_map/ppermute | solution.py:12
  21.8 2.3 %fusion.39 = f32[30,30]{1,0:T(8,128)S(1)} fusion(f32[30,6,8,3,128]{4,2,3,1,0:T(8,128)S(1)} %copy-done.1), kind=kOutput, calls=%fused_computation.76 | convolution fusion | flops 199065600 | bytes 2215440 | tf_op jit(solution)/shard_map/dot_general | solution.py:61
  24.9 2.6 %copy.340 = f32[30,6,8,3,128]{4,3,2,1,0:T(4,128)} copy(f32[30,6,8,3,128]{4,2,3,1,0:T(8,128)S(1)} %copy-done.1) | data formatting | bytes 4423680 | tf_op args[1]
  30.8 4.5 %reshape.317 = f32[30,18432]{1,0:T(8,128)} reshape(f32[30,6,8,3,128]{4,3,2,1,0:T(4,128)} %copy.340) | data formatting | bytes 4423680 | tf_op jit(solution)/shard_map/reshape | solution.py:57
  35.4 1.3 collective-permute-start.4
  36.7 1.3 collective-permute-start.5
  38.3 3.3 %collective-permute-done.5 = f32[6,18,1,128]{3,1,2,0:T(8,128)S(1)} collective-permute-done((f32[6,18,1,128]{3,1,2,0:T(8,128)S(1)}, f32[6,18,1,128]{3,1,2,0:T(8,128)S(1)}, u32[]{:S(2)}, u32[]{:S(2)}) %collective-permute-start.5) | collective-permute-done | bytes 55328 | tf_op jit(solution)/shard_map/ppermute | solution.py:15
  41.7 1.6 copy.319
  43.3 21.9 %collective-permute-done.2 = bf16[7,6,6,5,3,128]{5,0,4,3,2,1:T(8,128)(2,1)} collective-permute-done((bf16[7,6,6,5,3,128]{5,0,4,3,2,1:T(8,128)(2,1)}, bf16[7,6,6,5,3,128]{5,0,4,3,2,1:T(8,128)(2,1)}, u32[]{:S(2)}, u32[]{:S(2)}) %collective-permute-start.2) | collective-permute-done | bytes 967712 | tf_op jit(solution)/shard_map/ppermute | solution.py:12
  65.2 1.6 copy.318
  66.8 2.9 %pad_maximum_fusion = bf16[7,6,6,18,3,128]{5,3,4,2,1,0:T(8,128)(2,1)S(1)} fusion(bf16[7,6,6,5,3,128]{5,3,4,2,1,0:T(8,128)(2,1)S(1)} %copy.319, bf16[7,6,6,8,3,128]{5,3,4,2,1,0:T(8,128)(2,1)S(1)} %copy-done.2, bf16[7,6,6,5,3,128]{5,3,4,2,1,0:T(8,128)(2,1)S(1)} %copy.318), kind=kLoop, calls=%fused_computation.1 | loop fusion | flops 10450944 | bytes 6967296 | tf_op jit(solution)/shard_map/concatenate | solution.py:16
  69.7 1.1 fusion.4
  70.8 1.1 copy-done
  72.8 1.9 %collective-permute-start.6 = (f32[6,18,1,128]{3,1,2,0:T(8,128)}, f32[6,18,1,128]{3,1,2,0:T(8,128)S(1)}, u32[]{:S(2)}, u32[]{:S(2)}) collective-permute-start(f32[6,18,1,128]{3,1,2,0:T(8,128)} %get-tuple-element.102), channel_id=1, source_target_pairs={{0,1},{1,2},{2,3},{4,5},{5,6},{6,7},{8,9},{9,10},{10,11},{12,13},{... | collective-permute-start | bytes 165896 | tf_op jit(solution)/shard_map/ppermute | solution.py:12
  74.7 1.5 collective-permute-start.7
  76.2 0.7 stack.43
  77.2 1.7 collective-permute-done.7
  79.1 3.5 %fusion.5 = (f32[6,18,3,128]{3,1,2,0:T(8,128)S(1)}, f32[6,18,3,128]{3,1,2,0:T(8,128)S(1)}, f32[6,18,3,128]{3,1,2,0:T(8,128)S(1)}, f32[6,18,3,128]{3,1,2,0:T(8,12...) fusion(f32[6,18,3,128]{3,1,2,0:T(8,128)S(1)} %add_add_fusion.3, ...), kind=kLoop, calls=%fused_computation.42 | loop fusion | flops 4935168 | bytes 5806080 | tf_op jit(solution)/shard_map/reduce_sum | solution.py:40
  83.5 4.9 %collective-permute-start.8 = (f32[6,18,1,128]{3,1,2,0:T(8,128)}, f32[6,18,1,128]{3,1,2,0:T(8,128)S(1)}, u32[]{:S(2)}, u32[]{:S(2)}) collective-permute-start(f32[6,18,1,128]{3,1,2,0:T(8,128)} %get-tuple-element.96), channel_id=1, source_target_pairs={{0,1},{1,2},{2,3},{4,5},{5,6},{6,7},{8,9},{9,10},{10,11},{12,13},{... | collective-permute-start | bytes 165896 | tf_op jit(solution)/shard_map/ppermute | solution.py:12
  88.4 1.3 collective-permute-start.9
  89.8 0.7 stack.44
  90.7 1.0 collective-permute-done.9
  91.9 3.5 %fusion.6 = (f32[6,18,3,128]{3,1,2,0:T(8,128)S(1)}, f32[6,18,3,128]{3,1,2,0:T(8,128)S(1)}, f32[6,18,3,128]{3,1,2,0:T(8,128)S(1)}, f32[6,18,3,128]{3,1,2,0:T(8,12...) fusion(f32[6,18,3,128]{3,1,2,0:T(8,128)S(1)} %add_add_fusion.2, ...), kind=kLoop, calls=%fused_computation.43 | loop fusion | flops 4935168 | bytes 5806080 | tf_op jit(solution)/shard_map/reduce_sum | solution.py:40
  96.4 4.4 %collective-permute-start.10 = (f32[6,18,1,128]{3,1,2,0:T(8,128)}, f32[6,18,1,128]{3,1,2,0:T(8,128)S(1)}, u32[]{:S(2)}, u32[]{:S(2)}) collective-permute-start(f32[6,18,1,128]{3,1,2,0:T(8,128)} %get-tuple-element.90), channel_id=1, source_target_pairs={{0,1},{1,2},{2,3},{4,5},{5,6},{6,7},{8,9},{9,10},{10,11},{12,13},{... | collective-permute-start | bytes 165896 | tf_op jit(solution)/shard_map/ppermute | solution.py:12
  100.8 1.3 collective-permute-start.11
  102.8 0.7 stack.45
  103.7 1.0 copy.323
  104.8 3.5 %fusion.7 = (f32[6,18,3,128]{3,1,2,0:T(8,128)S(1)}, f32[6,18,3,128]{3,1,2,0:T(8,128)S(1)}, f32[6,18,3,128]{3,1,2,0:T(8,128)S(1)}, f32[6,18,3,128]{3,1,2,0:T(8,12...) fusion(f32[6,18,3,128]{3,1,2,0:T(8,128)S(1)} %add_add_fusion.1, ...), kind=kLoop, calls=%fused_computation.44 | loop fusion | flops 4935168 | bytes 5806080 | tf_op jit(solution)/shard_map/reduce_sum | solution.py:40
  109.3 4.0 %collective-permute-start.12 = (f32[6,18,1,128]{3,1,2,0:T(8,128)}, f32[6,18,1,128]{3,1,2,0:T(8,128)S(1)}, u32[]{:S(2)}, u32[]{:S(2)}) collective-permute-start(f32[6,18,1,128]{3,1,2,0:T(8,128)} %get-tuple-element.84), channel_id=1, source_target_pairs={{0,1},{1,2},{2,3},{4,5},{5,6},{6,7},{8,9},{9,10},{10,11},{12,13},{... | collective-permute-start | bytes 165896 | tf_op jit(solution)/shard_map/ppermute | solution.py:12
  113.3 1.3 collective-permute-start.13
  115.2 0.7 stack.46
  116.1 1.0 copy.324
  117.2 3.5 %fusion.8 = (f32[6,18,3,128]{3,1,2,0:T(8,128)S(1)}, f32[6,18,3,128]{3,1,2,0:T(8,128)S(1)}, f32[6,18,3,128]{3,1,2,0:T(8,128)S(1)}, f32[6,18,3,128]{3,1,2,0:T(8,12...) fusion(f32[6,18,3,128]{3,1,2,0:T(8,128)S(1)} %add_add_fusion, ...), kind=kLoop, calls=%fused_computation.45 | loop fusion | flops 4935168 | bytes 5806080 | tf_op jit(solution)/shard_map/reduce_sum | solution.py:40
  121.0 0.7 stack.41
  121.8 2.2 %fusion.42 = f32[30,6]{0,1:T(8,128)S(1)} fusion(f32[6,6,8,3,128]{4,0,3,2,1:T(8,128)S(1)} %stack.41, f32[30,6,8,3,128]{4,2,3,1,0:T(8,128)S(1)} %copy-done.1), kind=kOutput, calls=%fused_computation.77 | convolution fusion | flops 39813120 | bytes 2654928 | tf_op jit(solution)/shard_map/dot_general | solution.py:59
  124.0 1.4 convolution_bitcast_fusion
  125.5 42.9 %all-reduce.15 = (f32[30,6]{0,1:T(8,128)S(1)}, f32[6,6]{0,1:T(8,128)S(1)}, f32[30,30]{1,0:T(8,128)S(1)}) all-reduce(f32[30,6]{0,1:T(8,128)S(1)} %fusion.42, f32[6,6]{0,1:T(8,128)S(1)} %convolution_bitcast_fusion, f32[30,30]{1,0:T(8,128)S(1)} %fusion.39), channel_id=1, replica_groups=mesh['slab'=8,'sub'=4] {'slab','sub'}, use_global_device_ids=true, to_apply=%region_36.37 | all-reduce | flops 1116 | bytes 8928 | tf_op jit(solution)/shard_map/psum | solution.py:62
  171.3 0.7 stack.48
  172.1 2.9 %convolution_subtract_fusion = f32[6,18432]{1,0:T(8,128)S(1)} fusion(f32[6,18432]{1,0:T(8,128)S(1)} %stack.48, f32[30,6]{0,1:T(8,128)S(1)} %broadcast_multiply_fusion, f32[30,18432]{1,0:T(8,128)} %reshape.317), kind=kOutput, calls=%fused_computation | convolution fusion | flops 39923712 | bytes 3097296 | tf_op jit(solution)/shard_map/dot_general | solution.py:66
  175.0 0.8 fusion.50
  175.7 0.8 copy.342
  (99 shorter events, 11.5 us)
Async XLA Ops:
  1.6 33.7 %collective-permute-start.1 = (f32[6,5,3,128]{3,1,2,0:T(8,128)S(1)}, f32[6,5,3,128]{3,1,2,0:T(8,128)S(1)}, u32[]{:S(2)}, u32[]{:S(2)}) collective-permute-start(f32[6,5,3,128]{3,1,2,0:T(8,128)S(1)} %get-tuple-element.113), channel_id=1, source_target_pairs={{4,0},{8,4},{12,8},{16,12},{20,16},{24,20},{28,24},{5,1},{9,5},{13... | collective-permute-start | bytes 138248 | tf_op jit(solution)/shard_map/ppermute | solution.py:15
  2.9 32.4 %collective-permute-start = (f32[6,5,3,128]{3,1,2,0:T(8,128)S(1)}, f32[6,5,3,128]{3,1,2,0:T(8,128)S(1)}, u32[]{:S(2)}, u32[]{:S(2)}) collective-permute-start(f32[6,5,3,128]{3,1,2,0:T(8,128)S(1)} %get-tuple-element.112), channel_id=1, source_target_pairs={{0,4},{4,8},{8,12},{12,16},{16,20},{20,24},{24,28},{1,5},{5,9},{9,... | collective-permute-start | bytes 138248 | tf_op jit(solution)/shard_map/ppermute | solution.py:12
  12.4 29.3 %collective-permute-start.3 = (bf16[7,6,6,5,3,128]{5,0,4,3,2,1:T(8,128)(2,1)}, bf16[7,6,6,5,3,128]{5,0,4,3,2,1:T(8,128)(2,1)}, u32[]{:S(2)}, u32[]{:S(2)}) collective-permute-start(bf16[7,6,6,5,3,128]{5,0,4,3,2,1:T(8,128)(2,1)} %copy.352), channel_id=1, source_target_pairs={{4,0},{8,4},{12,8},{16,12},{20,16},{24,20},{28,24},{5,1},{9,5},{13... | collective-permute-start | bytes 2903048 | tf_op jit(solution)/shard_map/ppermute | solution.py:15
  13.7 8.1 %copy-start.1 = (f32[30,6,8,3,128]{4,2,3,1,0:T(8,128)S(1)}, f32[30,6,8,3,128]{4,2,3,1,0:T(8,128)}, u32[]{:S(2)}) copy-start(f32[30,6,8,3,128]{4,2,3,1,0:T(8,128)} %param.5) | copy-start | bytes 6635524
  15.2 8.9 %copy-start.9 = (f32[5]{0:T(128)S(1)}, f32[5]{0:T(128)}, u32[]{:S(2)}) copy-start(f32[5]{0:T(128)} %param.7) | copy-start | bytes 64
  15.2 9.6 %copy-start.3 = (f32[6,8,3,128]{3,1,2,0:T(8,128)S(1)}, f32[6,8,3,128]{3,1,2,0:T(8,128)}, u32[]{:S(2)}) copy-start(f32[6,8,3,128]{3,1,2,0:T(8,128)} %param.6) | copy-start | bytes 221188
  15.2 50.0 %collective-permute-start.2 = (bf16[7,6,6,5,3,128]{5,0,4,3,2,1:T(8,128)(2,1)}, bf16[7,6,6,5,3,128]{5,0,4,3,2,1:T(8,128)(2,1)}, u32[]{:S(2)}, u32[]{:S(2)}) collective-permute-start(bf16[7,6,6,5,3,128]{5,0,4,3,2,1:T(8,128)(2,1)} %copy.351), channel_id=1, source_target_pairs={{0,4},{4,8},{8,12},{12,16},{16,20},{20,24},{24,28},{1,5},{5,9},{9,... | collective-permute-start | bytes 2903048 | tf_op jit(solution)/shard_map/ppermute | solution.py:12
  35.4 2.9 %collective-permute-start.4 = (f32[6,18,1,128]{3,1,2,0:T(8,128)S(1)}, f32[6,18,1,128]{3,1,2,0:T(8,128)S(1)}, u32[]{:S(2)}, u32[]{:S(2)}) collective-permute-start(f32[6,18,1,128]{3,1,2,0:T(8,128)S(1)} %get-tuple-element.108), channel_id=1, source_target_pairs={{0,1},{1,2},{2,3},{4,5},{5,6},{6,7},{8,9},{9,10},{10,11},{12,13},{... | collective-permute-start | bytes 165896 | tf_op jit(solution)/shard_map/ppermute | solution.py:12
  36.7 4.9 %collective-permute-start.5 = (f32[6,18,1,128]{3,1,2,0:T(8,128)S(1)}, f32[6,18,1,128]{3,1,2,0:T(8,128)S(1)}, u32[]{:S(2)}, u32[]{:S(2)}) collective-permute-start(f32[6,18,1,128]{3,1,2,0:T(8,128)S(1)} %get-tuple-element.109), channel_id=1, source_target_pairs={{1,0},{2,1},{3,2},{5,4},{6,5},{7,6},{9,8},{10,9},{11,10},{13,12},{... | collective-permute-start | bytes 165896 | tf_op jit(solution)/shard_map/ppermute | solution.py:15
  43.3 23.5 %copy-start.2 = (bf16[7,6,6,8,3,128]{5,3,4,2,1,0:T(8,128)(2,1)S(1)}, bf16[7,6,6,8,3,128]{5,3,4,2,1,0:T(8,128)(2,1)}, u32[]{:S(2)}) copy-start(bf16[7,6,6,8,3,128]{5,3,4,2,1,0:T(8,128)(2,1)} %param.4) | copy-start | bytes 4644868
  69.7 2.2 %copy-start = (bf16[7,6,6,18,3,128]{5,3,4,2,1,0:T(8,128)(2,1)}, bf16[7,6,6,18,3,128]{5,3,4,2,1,0:T(8,128)(2,1)S(1)}, u32[]{:S(2)}) copy-start(bf16[7,6,6,18,3,128]{5,3,4,2,1,0:T(8,128)(2,1)S(1)} %pad_maximum_fusion) | copy-start | bytes 10450948
  72.8 4.4 %collective-permute-start.6 = (f32[6,18,1,128]{3,1,2,0:T(8,128)}, f32[6,18,1,128]{3,1,2,0:T(8,128)S(1)}, u32[]{:S(2)}, u32[]{:S(2)}) collective-permute-start(f32[6,18,1,128]{3,1,2,0:T(8,128)} %get-tuple-element.102), channel_id=1, source_target_pairs={{0,1},{1,2},{2,3},{4,5},{5,6},{6,7},{8,9},{9,10},{10,11},{12,13},{... | collective-permute-start | bytes 165896 | tf_op jit(solution)/shard_map/ppermute | solution.py:12
  74.7 4.3 %collective-permute-start.7 = (f32[6,18,1,128]{3,1,2,0:T(8,128)S(1)}, f32[6,18,1,128]{3,1,2,0:T(8,128)S(1)}, u32[]{:S(2)}, u32[]{:S(2)}) collective-permute-start(f32[6,18,1,128]{3,1,2,0:T(8,128)S(1)} %get-tuple-element.103), channel_id=1, source_target_pairs={{1,0},{2,1},{3,2},{5,4},{6,5},{7,6},{9,8},{10,9},{11,10},{13,12},{... | collective-permute-start | bytes 165896 | tf_op jit(solution)/shard_map/ppermute | solution.py:15
  83.5 7.2 %collective-permute-start.8 = (f32[6,18,1,128]{3,1,2,0:T(8,128)}, f32[6,18,1,128]{3,1,2,0:T(8,128)S(1)}, u32[]{:S(2)}, u32[]{:S(2)}) collective-permute-start(f32[6,18,1,128]{3,1,2,0:T(8,128)} %get-tuple-element.96), channel_id=1, source_target_pairs={{0,1},{1,2},{2,3},{4,5},{5,6},{6,7},{8,9},{9,10},{10,11},{12,13},{... | collective-permute-start | bytes 165896 | tf_op jit(solution)/shard_map/ppermute | solution.py:12
  88.4 3.4 %collective-permute-start.9 = (f32[6,18,1,128]{3,1,2,0:T(8,128)}, f32[6,18,1,128]{3,1,2,0:T(8,128)S(1)}, u32[]{:S(2)}, u32[]{:S(2)}) collective-permute-start(f32[6,18,1,128]{3,1,2,0:T(8,128)} %get-tuple-element.97), channel_id=1, source_target_pairs={{1,0},{2,1},{3,2},{5,4},{6,5},{7,6},{9,8},{10,9},{11,10},{13,12},{... | collective-permute-start | bytes 165896 | tf_op jit(solution)/shard_map/ppermute | solution.py:15
  96.4 8.2 %collective-permute-start.10 = (f32[6,18,1,128]{3,1,2,0:T(8,128)}, f32[6,18,1,128]{3,1,2,0:T(8,128)S(1)}, u32[]{:S(2)}, u32[]{:S(2)}) collective-permute-start(f32[6,18,1,128]{3,1,2,0:T(8,128)} %get-tuple-element.90), channel_id=1, source_target_pairs={{0,1},{1,2},{2,3},{4,5},{5,6},{6,7},{8,9},{9,10},{10,11},{12,13},{... | collective-permute-start | bytes 165896 | tf_op jit(solution)/shard_map/ppermute | solution.py:12
  100.8 3.8 %collective-permute-start.11 = (f32[6,18,1,128]{3,1,2,0:T(8,128)}, f32[6,18,1,128]{3,1,2,0:T(8,128)S(1)}, u32[]{:S(2)}, u32[]{:S(2)}) collective-permute-start(f32[6,18,1,128]{3,1,2,0:T(8,128)} %get-tuple-element.91), channel_id=1, source_target_pairs={{1,0},{2,1},{3,2},{5,4},{6,5},{7,6},{9,8},{10,9},{11,10},{13,12},{... | collective-permute-start | bytes 165896 | tf_op jit(solution)/shard_map/ppermute | solution.py:15
  109.3 7.8 %collective-permute-start.12 = (f32[6,18,1,128]{3,1,2,0:T(8,128)}, f32[6,18,1,128]{3,1,2,0:T(8,128)S(1)}, u32[]{:S(2)}, u32[]{:S(2)}) collective-permute-start(f32[6,18,1,128]{3,1,2,0:T(8,128)} %get-tuple-element.84), channel_id=1, source_target_pairs={{0,1},{1,2},{2,3},{4,5},{5,6},{6,7},{8,9},{9,10},{10,11},{12,13},{... | collective-permute-start | bytes 165896 | tf_op jit(solution)/shard_map/ppermute | solution.py:12
  113.3 3.8 %collective-permute-start.13 = (f32[6,18,1,128]{3,1,2,0:T(8,128)}, f32[6,18,1,128]{3,1,2,0:T(8,128)S(1)}, u32[]{:S(2)}, u32[]{:S(2)}) collective-permute-start(f32[6,18,1,128]{3,1,2,0:T(8,128)} %get-tuple-element.85), channel_id=1, source_target_pairs={{1,0},{2,1},{3,2},{5,4},{6,5},{7,6},{9,8},{10,9},{11,10},{13,12},{... | collective-permute-start | bytes 165896 | tf_op jit(solution)/shard_map/ppermute | solution.py:15
  124.0 47.3 %copy-start.4 = (f32[1,18432]{1,0:T(1,128)S(1)}, f32[1,18432]{1,0:T(1,128)}, u32[]{:S(2)}) copy-start(f32[1,18432]{1,0:T(1,128)} %stack.43) | copy-start | bytes 221188
  124.0 47.3 %copy-start.5 = (f32[1,18432]{1,0:T(1,128)S(1)}, f32[1,18432]{1,0:T(1,128)}, u32[]{:S(2)}) copy-start(f32[1,18432]{1,0:T(1,128)} %stack.44) | copy-start | bytes 221188
  124.0 47.3 %copy-start.6 = (f32[1,18432]{1,0:T(1,128)S(1)}, f32[1,18432]{1,0:T(1,128)}, u32[]{:S(2)}) copy-start(f32[1,18432]{1,0:T(1,128)} %stack.45) | copy-start | bytes 221188
  124.0 47.3 %copy-start.7 = (f32[1,18432]{1,0:T(1,128)S(1)}, f32[1,18432]{1,0:T(1,128)}, u32[]{:S(2)}) copy-start(f32[1,18432]{1,0:T(1,128)} %stack.46) | copy-start | bytes 221188
  168.4 6.5 %copy-start.8 = (f32[30,6]{0,1:T(8,128)}, f32[30,6]{0,1:T(8,128)S(1)}, u32[]{:S(2)}) copy-start(f32[30,6]{0,1:T(8,128)S(1)} %broadcast_multiply_fusion) | copy-start | bytes 2164
where the time goes:
time: 178 us; the launch traced here: 177 us
  blocking collectives  42.9 us (24%)
  starting transfers between devices  37.9 us (21%)
  local copies, waits for them, and re-layouts  32.4 us (18%)
  waiting for transfers between devices  28 us (16%)
  other arithmetic  21.6 us (12%)
  matrix products  9.97 us (6%)
  between operations  4.5 us (3%)
    psum x1, blocking collectives, body(): lax.psum((local_cross, local_self, local_earlier), ('slab', 'sub'))  42.9 us
    ppermute x7, starting transfers between devices, padded_2(): lax.ppermute(lax.slice_in_dim(block, block.shape[dim] - width, None, axis...  28.7 us
    ppermute x7, waiting for transfers between devices, padded_2(): lax.ppermute(lax.slice_in_dim(block, block.shape[dim] - width, None, axis...  21.9 us
    reduce_sum x5, other arithmetic, apply_padded(): jnp.sum(coefficients[coupling] * fields[coupling][None], axis=1)  15.2 us
    ppermute x7, starting transfers between devices, padded_2(): lax.ppermute(lax.slice_in_dim(block, 0, width, axis=dim), axis, backward)  9.21 us
    unnamed x26, local copies, waits for them, and re-layouts  8.24 us
    another operation x18, local copies, waits for them, and re-layouts, body(): basis = jnp.stack(vectors)  8.1 us
    slice x7, local copies, waits for them, and re-layouts, padded_2(): lax.slice_in_dim(block, block.shape[dim] - width, None, axis=dim)  6.15 us
  transfers between devices with their start and end apart: 14, of which 4 were waited for; matrix products, arithmetic and copies ran while one was open for 14% of the time, Pallas kernels for 0%

commit v1 on v0

--- a/solution.py
+++ b/solution.py
@@ -2,6 +2,11 @@
 import jax.numpy as jnp
 from jax import lax
 from jax.sharding import PartitionSpec as P
+
+
+def run_group_on(own_rows):
+    parts_out = lax.psum(own_rows, "sub")
+    return lax.psum(parts_out, "slab")
 
 
 def padded_2(block, sides, width):
@@ -59,9 +64,7 @@
     local_cross = jnp.dot(earlier_flat, flat.T, precision=lax.Precision.HIGHEST)
     local_self = jnp.dot(flat, flat.T, precision=lax.Precision.HIGHEST)
     local_earlier = jnp.dot(earlier_flat, earlier_flat.T, precision=lax.Precision.HIGHEST)
-    cross_sum, self_sum, earlier_sum = lax.psum(
-        (local_cross, local_self, local_earlier), ("slab", "sub")
-    )
+    cross_sum, self_sum, earlier_sum = run_group_on((local_cross, local_self, local_earlier))
     projection = cross_sum / count
     rest = flat - jnp.dot(projection.T, earlier_flat, precision=lax.Precision.HIGHEST)
     weighted = jnp.dot(earlier_sum / count, projection, precision=lax.Precision.HIGHEST)

time: 178 us -> 184 us (1.034)
  blocking collectives: 42.9 us -> 48.8 us
    psum x1 -> x2, blocking collectives: 42.9 us -> 48.8 us  [the longest x1 36.3 us: run_group_on(): return lax.psum(parts_out, 'slab')]
  transfers between devices with their start and end apart: 14 -> 14, of which waited for: 4 -> 4; matrix products, arithmetic and copies ran while one was open for 14% -> 13% of each run, Pallas kernels for 0% -> 0%
where the time goes in v1:
time: 184 us; the launch traced here: 183 us
  blocking collectives  48.8 us (27%)
  starting transfers between devices  37.9 us (21%)
  local copies, waits for them, and re-layouts  32.4 us (18%)
  waiting for transfers between devices  28 us (15%)
  other arithmetic  21.6 us (12%)
  matrix products  9.97 us (5%)
  between operations  4.49 us (2%)
    psum x1, blocking collectives, run_group_on(): return lax.psum(parts_out, 'slab')  36.3 us
    ppermute x7, starting transfers between devices, padded_2(): lax.ppermute(lax.slice_in_dim(block, block.shape[dim] - width, None, axis...  28.7 us
    ppermute x7, waiting for transfers between devices, padded_2(): lax.ppermute(lax.slice_in_dim(block, block.shape[dim] - width, None, axis...  21.9 us
    reduce_sum x5, other arithmetic, apply_padded(): jnp.sum(coefficients[coupling] * fields[coupling][None], axis=1)  15.2 us
    psum x1, blocking collectives, run_group_on(): parts_out = lax.psum(own_rows, 'sub')  12.5 us
    ppermute x7, starting transfers between devices, padded_2(): lax.ppermute(lax.slice_in_dim(block, 0, width, axis=dim), axis, backward)  9.21 us
    unnamed x26, local copies, waits for them, and re-layouts  8.24 us
    another operation x18, local copies, waits for them, and re-layouts, body(): basis = jnp.stack(vectors)  8.1 us
  transfers between devices with their start and end apart: 14, of which 4 were waited for; matrix products, arithmetic and copies ran while one was open for 13% of the time, Pallas kernels for 0%

profile of v1, /device:TPU:0, one launch (start us, length us, event | category | flops | bytes accessed | tf_op | source)
XLA Modules:
  0.0 183.1 jit_solution(9244571424164511415)
XLA Ops:
  0.6 1.0 fusion.71
  1.6 1.3 collective-permute-start.1
  2.9 5.5 %collective-permute-start = (f32[6,5,3,128]{3,1,2,0:T(8,128)S(1)}, f32[6,5,3,128]{3,1,2,0:T(8,128)S(1)}, u32[]{:S(2)}, u32[]{:S(2)}) collective-permute-start(f32[6,5,3,128]{3,1,2,0:T(8,128)S(1)} %get-tuple-element.115), channel_id=1, source_target_pairs={{0,4},{4,8},{8,12},{12,16},{16,20},{20,24},{24,28},{1,5},{5,9},{9,... | collective-permute-start | bytes 138248 | tf_op jit(solution)/shard_map/ppermute | solution.py:17
  8.4 2.5 %fusion.55 = (bf16[7,6,6,5,3,128]{5,3,4,2,1,0:T(8,128)(2,1)S(1)}, bf16[7,6,6,5,3,128]{5,3,4,2,1,0:T(8,128)(2,1)S(1)}) fusion(bf16[7,6,6,8,3,128]{5,3,4,2,1,0:T(8,128)(2,1)} %param.4), kind=kLoop, calls=%fused_computation.150 | loop fusion | bytes 3870720 | tf_op jit(solution)/shard_map/slice | solution.py:18
  10.9 1.5 copy.352
  12.4 1.3 collective-permute-start.3
  13.7 1.5 copy.351
  15.2 6.6 %collective-permute-start.2 = (bf16[7,6,6,5,3,128]{5,0,4,3,2,1:T(8,128)(2,1)}, bf16[7,6,6,5,3,128]{5,0,4,3,2,1:T(8,128)(2,1)}, u32[]{:S(2)}, u32[]{:S(2)}) collective-permute-start(bf16[7,6,6,5,3,128]{5,0,4,3,2,1:T(8,128)(2,1)} %copy.351), channel_id=1, source_target_pairs={{0,4},{4,8},{8,12},{12,16},{16,20},{20,24},{24,28},{1,5},{5,9},{9,... | collective-permute-start | bytes 2903048 | tf_op jit(solution)/shard_map/ppermute | solution.py:17
  21.8 2.3 %fusion.39 = f32[30,30]{1,0:T(8,128)S(1)} fusion(f32[30,6,8,3,128]{4,2,3,1,0:T(8,128)S(1)} %copy-done.1), kind=kOutput, calls=%fused_computation.76 | convolution fusion | flops 199065600 | bytes 2215440 | tf_op jit(solution)/shard_map/dot_general | solution.py:66
  24.9 2.6 %copy.340 = f32[30,6,8,3,128]{4,3,2,1,0:T(4,128)} copy(f32[30,6,8,3,128]{4,2,3,1,0:T(8,128)S(1)} %copy-done.1) | data formatting | bytes 4423680 | tf_op args[1]
  30.8 4.5 %reshape.317 = f32[30,18432]{1,0:T(8,128)} reshape(f32[30,6,8,3,128]{4,3,2,1,0:T(4,128)} %copy.340) | data formatting | bytes 4423680 | tf_op jit(solution)/shard_map/reshape | solution.py:62
  35.4 1.3 collective-permute-start.4
  36.7 1.3 collective-permute-start.5
  38.3 3.3 %collective-permute-done.5 = f32[6,18,1,128]{3,1,2,0:T(8,128)S(1)} collective-permute-done((f32[6,18,1,128]{3,1,2,0:T(8,128)S(1)}, f32[6,18,1,128]{3,1,2,0:T(8,128)S(1)}, u32[]{:S(2)}, u32[]{:S(2)}) %collective-permute-start.5) | collective-permute-done | bytes 55328 | tf_op jit(solution)/shard_map/ppermute | solution.py:20
  41.7 1.6 copy.319
  43.3 21.9 %collective-permute-done.2 = bf16[7,6,6,5,3,128]{5,0,4,3,2,1:T(8,128)(2,1)} collective-permute-done((bf16[7,6,6,5,3,128]{5,0,4,3,2,1:T(8,128)(2,1)}, bf16[7,6,6,5,3,128]{5,0,4,3,2,1:T(8,128)(2,1)}, u32[]{:S(2)}, u32[]{:S(2)}) %collective-permute-start.2) | collective-permute-done | bytes 967712 | tf_op jit(solution)/shard_map/ppermute | solution.py:17
  65.2 1.6 copy.318
  66.8 2.9 %pad_maximum_fusion = bf16[7,6,6,18,3,128]{5,3,4,2,1,0:T(8,128)(2,1)S(1)} fusion(bf16[7,6,6,5,3,128]{5,3,4,2,1,0:T(8,128)(2,1)S(1)} %copy.319, bf16[7,6,6,8,3,128]{5,3,4,2,1,0:T(8,128)(2,1)S(1)} %copy-done.2, bf16[7,6,6,5,3,128]{5,3,4,2,1,0:T(8,128)(2,1)S(1)} %copy.318), kind=kLoop, calls=%fused_computation.1 | loop fusion | flops 10450944 | bytes 6967296 | tf_op jit(solution)/shard_map/concatenate | solution.py:21
  69.7 1.1 fusion.4
  70.8 1.1 copy-done
  72.8 1.9 %collective-permute-start.6 = (f32[6,18,1,128]{3,1,2,0:T(8,128)}, f32[6,18,1,128]{3,1,2,0:T(8,128)S(1)}, u32[]{:S(2)}, u32[]{:S(2)}) collective-permute-start(f32[6,18,1,128]{3,1,2,0:T(8,128)} %get-tuple-element.105), channel_id=1, source_target_pairs={{0,1},{1,2},{2,3},{4,5},{5,6},{6,7},{8,9},{9,10},{10,11},{12,13},{... | collective-permute-start | bytes 165896 | tf_op jit(solution)/shard_map/ppermute | solution.py:17
  74.7 1.5 collective-permute-start.7
  76.2 0.7 stack.43
  77.2 1.7 collective-permute-done.7
  79.1 3.5 %fusion.5 = (f32[6,18,3,128]{3,1,2,0:T(8,128)S(1)}, f32[6,18,3,128]{3,1,2,0:T(8,128)S(1)}, f32[6,18,3,128]{3,1,2,0:T(8,128)S(1)}, f32[6,18,3,128]{3,1,2,0:T(8,12...) fusion(f32[6,18,3,128]{3,1,2,0:T(8,128)S(1)} %add_add_fusion.3, ...), kind=kLoop, calls=%fused_computation.42 | loop fusion | flops 4935168 | bytes 5806080 | tf_op jit(solution)/shard_map/reduce_sum | solution.py:45
  83.5 4.9 %collective-permute-start.8 = (f32[6,18,1,128]{3,1,2,0:T(8,128)}, f32[6,18,1,128]{3,1,2,0:T(8,128)S(1)}, u32[]{:S(2)}, u32[]{:S(2)}) collective-permute-start(f32[6,18,1,128]{3,1,2,0:T(8,128)} %get-tuple-element.99), channel_id=1, source_target_pairs={{0,1},{1,2},{2,3},{4,5},{5,6},{6,7},{8,9},{9,10},{10,11},{12,13},{... | collective-permute-start | bytes 165896 | tf_op jit(solution)/shard_map/ppermute | solution.py:17
  88.4 1.3 collective-permute-start.9
  89.8 0.7 stack.44
  90.7 1.0 collective-permute-done.9
  91.9 3.5 %fusion.6 = (f32[6,18,3,128]{3,1,2,0:T(8,128)S(1)}, f32[6,18,3,128]{3,1,2,0:T(8,128)S(1)}, f32[6,18,3,128]{3,1,2,0:T(8,128)S(1)}, f32[6,18,3,128]{3,1,2,0:T(8,12...) fusion(f32[6,18,3,128]{3,1,2,0:T(8,128)S(1)} %add_add_fusion.2, ...), kind=kLoop, calls=%fused_computation.43 | loop fusion | flops 4935168 | bytes 5806080 | tf_op jit(solution)/shard_map/reduce_sum | solution.py:45
  96.4 4.4 %collective-permute-start.10 = (f32[6,18,1,128]{3,1,2,0:T(8,128)}, f32[6,18,1,128]{3,1,2,0:T(8,128)S(1)}, u32[]{:S(2)}, u32[]{:S(2)}) collective-permute-start(f32[6,18,1,128]{3,1,2,0:T(8,128)} %get-tuple-element.93), channel_id=1, source_target_pairs={{0,1},{1,2},{2,3},{4,5},{5,6},{6,7},{8,9},{9,10},{10,11},{12,13},{... | collective-permute-start | bytes 165896 | tf_op jit(solution)/shard_map/ppermute | solution.py:17
  100.8 1.3 collective-permute-start.11
  103.7 1.0 copy.323
  104.8 3.5 %fusion.7 = (f32[6,18,3,128]{3,1,2,0:T(8,128)S(1)}, f32[6,18,3,128]{3,1,2,0:T(8,128)S(1)}, f32[6,18,3,128]{3,1,2,0:T(8,128)S(1)}, f32[6,18,3,128]{3,1,2,0:T(8,12...) fusion(f32[6,18,3,128]{3,1,2,0:T(8,128)S(1)} %add_add_fusion.1, ...), kind=kLoop, calls=%fused_computation.44 | loop fusion | flops 4935168 | bytes 5806080 | tf_op jit(solution)/shard_map/reduce_sum | solution.py:45
  109.3 4.0 %collective-permute-start.12 = (f32[6,18,1,128]{3,1,2,0:T(8,128)}, f32[6,18,1,128]{3,1,2,0:T(8,128)S(1)}, u32[]{:S(2)}, u32[]{:S(2)}) collective-permute-start(f32[6,18,1,128]{3,1,2,0:T(8,128)} %get-tuple-element.87), channel_id=1, source_target_pairs={{0,1},{1,2},{2,3},{4,5},{5,6},{6,7},{8,9},{9,10},{10,11},{12,13},{... | collective-permute-start | bytes 165896 | tf_op jit(solution)/shard_map/ppermute | solution.py:17
  113.3 1.3 collective-permute-start.13
  115.2 0.7 stack.46
  116.1 1.0 copy.324
  117.2 3.5 %fusion.8 = (f32[6,18,3,128]{3,1,2,0:T(8,128)S(1)}, f32[6,18,3,128]{3,1,2,0:T(8,128)S(1)}, f32[6,18,3,128]{3,1,2,0:T(8,128)S(1)}, f32[6,18,3,128]{3,1,2,0:T(8,12...) fusion(f32[6,18,3,128]{3,1,2,0:T(8,128)S(1)} %add_add_fusion, ...), kind=kLoop, calls=%fused_computation.45 | loop fusion | flops 4935168 | bytes 5806080 | tf_op jit(solution)/shard_map/reduce_sum | solution.py:45
  121.0 0.7 stack.41
  121.8 2.2 %fusion.42 = f32[30,6]{0,1:T(8,128)S(1)} fusion(f32[6,6,8,3,128]{4,0,3,2,1:T(8,128)S(1)} %stack.41, f32[30,6,8,3,128]{4,2,3,1,0:T(8,128)S(1)} %copy-done.1), kind=kOutput, calls=%fused_computation.77 | convolution fusion | flops 39813120 | bytes 2654928 | tf_op jit(solution)/shard_map/dot_general | solution.py:64
  124.0 1.4 convolution_bitcast_fusion
  125.5 12.5 %all-reduce.16 = (f32[30,6]{0,1:T(8,128)S(1)}, f32[6,6]{0,1:T(8,128)S(1)}, f32[30,30]{1,0:T(8,128)S(1)}) all-reduce(f32[30,6]{0,1:T(8,128)S(1)} %fusion.42, f32[6,6]{0,1:T(8,128)S(1)} %convolution_bitcast_fusion, f32[30,30]{1,0:T(8,128)S(1)} %fusion.39), channel_id=1, replica_groups=mesh['slab'=8,'sub'=4] {'sub'}, use_global_device_ids=true, to_apply=%region_37.38 | all-reduce | flops 1116 | bytes 8928 | tf_op jit(solution)/shard_map/psum | solution.py:8
  138.0 36.3 %all-reduce.15 = (f32[30,6]{0,1:T(8,128)S(1)}, f32[6,6]{0,1:T(8,128)S(1)}, f32[30,30]{1,0:T(8,128)S(1)}) all-reduce(f32[30,6]{0,1:T(8,128)S(1)} %get-tuple-element.62, f32[6,6]{0,1:T(8,128)S(1)} %get-tuple-element.63, f32[30,30]{1,0:T(8,128)S(1)} %get-tuple-element.64), channel_id=1, replica_groups=mesh['slab'=8,'sub'=4] {'slab'}, use_global_device_ids=true, to_apply=%region_38.39 | all-reduce | flops 1116 | bytes 8928 | tf_op jit(solution)/shard_map/psum | solution.py:9
  177.2 0.7 stack.48
  177.9 2.9 %convolution_subtract_fusion = f32[6,18432]{1,0:T(8,128)S(1)} fusion(f32[6,18432]{1,0:T(8,128)S(1)} %stack.48, f32[30,6]{0,1:T(8,128)S(1)} %broadcast_multiply_fusion, f32[30,18432]{1,0:T(8,128)} %reshape.317), kind=kOutput, calls=%fused_computation | convolution fusion | flops 39923712 | bytes 3097296 | tf_op jit(solution)/shard_map/dot_general | solution.py:69
  180.8 0.8 fusion.50
  181.6 0.8 copy.342
  (100 shorter events, 12.2 us)
Async XLA Ops:
  1.6 33.7 %collective-permute-start.1 = (f32[6,5,3,128]{3,1,2,0:T(8,128)S(1)}, f32[6,5,3,128]{3,1,2,0:T(8,128)S(1)}, u32[]{:S(2)}, u32[]{:S(2)}) collective-permute-start(f32[6,5,3,128]{3,1,2,0:T(8,128)S(1)} %get-tuple-element.116), channel_id=1, source_target_pairs={{4,0},{8,4},{12,8},{16,12},{20,16},{24,20},{28,24},{5,1},{9,5},{13... | collective-permute-start | bytes 138248 | tf_op jit(solution)/shard_map/ppermute | solution.py:20
  2.9 32.4 %collective-permute-start = (f32[6,5,3,128]{3,1,2,0:T(8,128)S(1)}, f32[6,5,3,128]{3,1,2,0:T(8,128)S(1)}, u32[]{:S(2)}, u32[]{:S(2)}) collective-permute-start(f32[6,5,3,128]{3,1,2,0:T(8,128)S(1)} %get-tuple-element.115), channel_id=1, source_target_pairs={{0,4},{4,8},{8,12},{12,16},{16,20},{20,24},{24,28},{1,5},{5,9},{9,... | collective-permute-start | bytes 138248 | tf_op jit(solution)/shard_map/ppermute | solution.py:17
  12.4 29.3 %collective-permute-start.3 = (bf16[7,6,6,5,3,128]{5,0,4,3,2,1:T(8,128)(2,1)}, bf16[7,6,6,5,3,128]{5,0,4,3,2,1:T(8,128)(2,1)}, u32[]{:S(2)}, u32[]{:S(2)}) collective-permute-start(bf16[7,6,6,5,3,128]{5,0,4,3,2,1:T(8,128)(2,1)} %copy.352), channel_id=1, source_target_pairs={{4,0},{8,4},{12,8},{16,12},{20,16},{24,20},{28,24},{5,1},{9,5},{13... | collective-permute-start | bytes 2903048 | tf_op jit(solution)/shard_map/ppermute | solution.py:20
  13.7 8.1 %copy-start.1 = (f32[30,6,8,3,128]{4,2,3,1,0:T(8,128)S(1)}, f32[30,6,8,3,128]{4,2,3,1,0:T(8,128)}, u32[]{:S(2)}) copy-start(f32[30,6,8,3,128]{4,2,3,1,0:T(8,128)} %param.5) | copy-start | bytes 6635524
  15.2 8.9 %copy-start.9 = (f32[5]{0:T(128)S(1)}, f32[5]{0:T(128)}, u32[]{:S(2)}) copy-start(f32[5]{0:T(128)} %param.7) | copy-start | bytes 64
  15.2 9.6 %copy-start.3 = (f32[6,8,3,128]{3,1,2,0:T(8,128)S(1)}, f32[6,8,3,128]{3,1,2,0:T(8,128)}, u32[]{:S(2)}) copy-start(f32[6,8,3,128]{3,1,2,0:T(8,128)} %param.6) | copy-start | bytes 221188
  15.2 50.0 %collective-permute-start.2 = (bf16[7,6,6,5,3,128]{5,0,4,3,2,1:T(8,128)(2,1)}, bf16[7,6,6,5,3,128]{5,0,4,3,2,1:T(8,128)(2,1)}, u32[]{:S(2)}, u32[]{:S(2)}) collective-permute-start(bf16[7,6,6,5,3,128]{5,0,4,3,2,1:T(8,128)(2,1)} %copy.351), channel_id=1, source_target_pairs={{0,4},{4,8},{8,12},{12,16},{16,20},{20,24},{24,28},{1,5},{5,9},{9,... | collective-permute-start | bytes 2903048 | tf_op jit(solution)/shard_map/ppermute | solution.py:17
  35.4 2.9 %collective-permute-start.4 = (f32[6,18,1,128]{3,1,2,0:T(8,128)S(1)}, f32[6,18,1,128]{3,1,2,0:T(8,128)S(1)}, u32[]{:S(2)}, u32[]{:S(2)}) collective-permute-start(f32[6,18,1,128]{3,1,2,0:T(8,128)S(1)} %get-tuple-element.111), channel_id=1, source_target_pairs={{0,1},{1,2},{2,3},{4,5},{5,6},{6,7},{8,9},{9,10},{10,11},{12,13},{... | collective-permute-start | bytes 165896 | tf_op jit(solution)/shard_map/ppermute | solution.py:17
  36.7 4.9 %collective-permute-start.5 = (f32[6,18,1,128]{3,1,2,0:T(8,128)S(1)}, f32[6,18,1,128]{3,1,2,0:T(8,128)S(1)}, u32[]{:S(2)}, u32[]{:S(2)}) collective-permute-start(f32[6,18,1,128]{3,1,2,0:T(8,128)S(1)} %get-tuple-element.112), channel_id=1, source_target_pairs={{1,0},{2,1},{3,2},{5,4},{6,5},{7,6},{9,8},{10,9},{11,10},{13,12},{... | collective-permute-start | bytes 165896 | tf_op jit(solution)/shard_map/ppermute | solution.py:20
  43.3 23.5 %copy-start.2 = (bf16[7,6,6,8,3,128]{5,3,4,2,1,0:T(8,128)(2,1)S(1)}, bf16[7,6,6,8,3,128]{5,3,4,2,1,0:T(8,128)(2,1)}, u32[]{:S(2)}) copy-start(bf16[7,6,6,8,3,128]{5,3,4,2,1,0:T(8,128)(2,1)} %param.4) | copy-start | bytes 4644868
  69.7 2.2 %copy-start = (bf16[7,6,6,18,3,128]{5,3,4,2,1,0:T(8,128)(2,1)}, bf16[7,6,6,18,3,128]{5,3,4,2,1,0:T(8,128)(2,1)S(1)}, u32[]{:S(2)}) copy-start(bf16[7,6,6,18,3,128]{5,3,4,2,1,0:T(8,128)(2,1)S(1)} %pad_maximum_fusion) | copy-start | bytes 10450948
  72.8 4.4 %collective-permute-start.6 = (f32[6,18,1,128]{3,1,2,0:T(8,128)}, f32[6,18,1,128]{3,1,2,0:T(8,128)S(1)}, u32[]{:S(2)}, u32[]{:S(2)}) collective-permute-start(f32[6,18,1,128]{3,1,2,0:T(8,128)} %get-tuple-element.105), channel_id=1, source_target_pairs={{0,1},{1,2},{2,3},{4,5},{5,6},{6,7},{8,9},{9,10},{10,11},{12,13},{... | collective-permute-start | bytes 165896 | tf_op jit(solution)/shard_map/ppermute | solution.py:17
  74.7 4.3 %collective-permute-start.7 = (f32[6,18,1,128]{3,1,2,0:T(8,128)S(1)}, f32[6,18,1,128]{3,1,2,0:T(8,128)S(1)}, u32[]{:S(2)}, u32[]{:S(2)}) collective-permute-start(f32[6,18,1,128]{3,1,2,0:T(8,128)S(1)} %get-tuple-element.106), channel_id=1, source_target_pairs={{1,0},{2,1},{3,2},{5,4},{6,5},{7,6},{9,8},{10,9},{11,10},{13,12},{... | collective-permute-start | bytes 165896 | tf_op jit(solution)/shard_map/ppermute | solution.py:20
  83.5 7.2 %collective-permute-start.8 = (f32[6,18,1,128]{3,1,2,0:T(8,128)}, f32[6,18,1,128]{3,1,2,0:T(8,128)S(1)}, u32[]{:S(2)}, u32[]{:S(2)}) collective-permute-start(f32[6,18,1,128]{3,1,2,0:T(8,128)} %get-tuple-element.99), channel_id=1, source_target_pairs={{0,1},{1,2},{2,3},{4,5},{5,6},{6,7},{8,9},{9,10},{10,11},{12,13},{... | collective-permute-start | bytes 165896 | tf_op jit(solution)/shard_map/ppermute | solution.py:17
  88.4 3.4 %collective-permute-start.9 = (f32[6,18,1,128]{3,1,2,0:T(8,128)}, f32[6,18,1,128]{3,1,2,0:T(8,128)S(1)}, u32[]{:S(2)}, u32[]{:S(2)}) collective-permute-start(f32[6,18,1,128]{3,1,2,0:T(8,128)} %get-tuple-element.100), channel_id=1, source_target_pairs={{1,0},{2,1},{3,2},{5,4},{6,5},{7,6},{9,8},{10,9},{11,10},{13,12},{... | collective-permute-start | bytes 165896 | tf_op jit(solution)/shard_map/ppermute | solution.py:20
  96.4 8.2 %collective-permute-start.10 = (f32[6,18,1,128]{3,1,2,0:T(8,128)}, f32[6,18,1,128]{3,1,2,0:T(8,128)S(1)}, u32[]{:S(2)}, u32[]{:S(2)}) collective-permute-start(f32[6,18,1,128]{3,1,2,0:T(8,128)} %get-tuple-element.93), channel_id=1, source_target_pairs={{0,1},{1,2},{2,3},{4,5},{5,6},{6,7},{8,9},{9,10},{10,11},{12,13},{... | collective-permute-start | bytes 165896 | tf_op jit(solution)/shard_map/ppermute | solution.py:17
  100.8 3.8 %collective-permute-start.11 = (f32[6,18,1,128]{3,1,2,0:T(8,128)}, f32[6,18,1,128]{3,1,2,0:T(8,128)S(1)}, u32[]{:S(2)}, u32[]{:S(2)}) collective-permute-start(f32[6,18,1,128]{3,1,2,0:T(8,128)} %get-tuple-element.94), channel_id=1, source_target_pairs={{1,0},{2,1},{3,2},{5,4},{6,5},{7,6},{9,8},{10,9},{11,10},{13,12},{... | collective-permute-start | bytes 165896 | tf_op jit(solution)/shard_map/ppermute | solution.py:20
  109.3 7.8 %collective-permute-start.12 = (f32[6,18,1,128]{3,1,2,0:T(8,128)}, f32[6,18,1,128]{3,1,2,0:T(8,128)S(1)}, u32[]{:S(2)}, u32[]{:S(2)}) collective-permute-start(f32[6,18,1,128]{3,1,2,0:T(8,128)} %get-tuple-element.87), channel_id=1, source_target_pairs={{0,1},{1,2},{2,3},{4,5},{5,6},{6,7},{8,9},{9,10},{10,11},{12,13},{... | collective-permute-start | bytes 165896 | tf_op jit(solution)/shard_map/ppermute | solution.py:17
  113.3 3.8 %collective-permute-start.13 = (f32[6,18,1,128]{3,1,2,0:T(8,128)}, f32[6,18,1,128]{3,1,2,0:T(8,128)S(1)}, u32[]{:S(2)}, u32[]{:S(2)}) collective-permute-start(f32[6,18,1,128]{3,1,2,0:T(8,128)} %get-tuple-element.88), channel_id=1, source_target_pairs={{1,0},{2,1},{3,2},{5,4},{6,5},{7,6},{9,8},{10,9},{11,10},{13,12},{... | collective-permute-start | bytes 165896 | tf_op jit(solution)/shard_map/ppermute | solution.py:20
  124.0 53.2 %copy-start.4 = (f32[1,18432]{1,0:T(1,128)S(1)}, f32[1,18432]{1,0:T(1,128)}, u32[]{:S(2)}) copy-start(f32[1,18432]{1,0:T(1,128)} %stack.43) | copy-start | bytes 221188
  124.0 53.2 %copy-start.5 = (f32[1,18432]{1,0:T(1,128)S(1)}, f32[1,18432]{1,0:T(1,128)}, u32[]{:S(2)}) copy-start(f32[1,18432]{1,0:T(1,128)} %stack.44) | copy-start | bytes 221188
  124.0 53.2 %copy-start.6 = (f32[1,18432]{1,0:T(1,128)S(1)}, f32[1,18432]{1,0:T(1,128)}, u32[]{:S(2)}) copy-start(f32[1,18432]{1,0:T(1,128)} %stack.45) | copy-start | bytes 221188
  124.0 53.2 %copy-start.7 = (f32[1,18432]{1,0:T(1,128)S(1)}, f32[1,18432]{1,0:T(1,128)}, u32[]{:S(2)}) copy-start(f32[1,18432]{1,0:T(1,128)} %stack.46) | copy-start | bytes 221188
  174.3 6.5 %copy-start.8 = (f32[30,6]{0,1:T(8,128)}, f32[30,6]{0,1:T(8,128)S(1)}, u32[]{:S(2)}) copy-start(f32[30,6]{0,1:T(8,128)S(1)} %broadcast_multiply_fusion) | copy-start | bytes 2164
